TPU v7x, 32 devices: a whole 2x2x4 slice. The times are simulated.
32 devices in a mesh: kpt: 4 (over y, core), row: 4 (over z), col: 2 (over x).
Axes of the slice: x: 2, y: 2, z: 4, core: 2. Of those that a mesh axis runs over, the one named last changes fastest.
Arguments:
- a_matrix: bfloat16 [8, 4096, 4096], P('kpt', 'row', 'col'), parts along dimension 0, may hold values from -6 to 6
- b_matrix: bfloat16 [8, 4096, 4096], P('kpt', 'row', 'col'), parts along dimension 0, may hold values from -0.09375 to 0.09375
- a_level: int32 [128, 32], P('kpt'), parts along dimension 0, may hold values from 0 to 4, as said below
- b_level: int32 [128, 32], P('kpt'), parts along dimension 0, may hold values from 0 to 4, as said below
- limit: int32 [128, 32], P(('kpt', 'row'), 'col'), parts along dimension 0, may hold values from 3 to 8
Outputs:
- product: bfloat16 [8, 4096, 4096], P('kpt', 'row', 'col'), parts along dimension 0
- kept_count: int32 [128, 32], P(('kpt', 'row'), 'col'), parts along dimension 0
- kept_total: int32 [4], P('kpt'), parts along dimension 0
There are 4 independent parts, one for each index of `kpt`. A program takes and returns all parts, laid end to end along the dimension named above; each array names one. Nothing has to cross between parts.
Inputs may be any that keep to these rules, and one draw needn't show every extreme that they name: Each block's level is 0 (empty) or its norm exponent 1 to 4; the share of occupied blocks rises from some a sixth in the first block row of a_level (block column of b_level) to some six in seven in the last. `b_level`: as for a_level, with the share rising along block columns.
All inputs are finite; a program needn't handle non-finite values.
Results may differ from a plain program's by a relative error of at most 0.001.
Values may be sent and summed in bfloat16 or wider, within the bound.
No kernel may reach another device: no remote copies, remote signals or barrier semaphores. Data moves between devices by JAX's collectives and lax.ppermute only.
A program may use at most 576 MiB of HBM per device.

v0:
```python
import jax
import jax.numpy as jnp
from jax import lax
from jax.sharding import PartitionSpec as P

BLK = 128


def level_scale(levels):
    power = jnp.power(jnp.float32(2.0), (1 - levels).astype(jnp.float32))
    return jnp.where(levels > 0, power, jnp.float32(0.0))


def spread_blocks(small):
    return jnp.repeat(jnp.repeat(small, BLK, axis=0), BLK, axis=1)


def block_terms(a_piece, a_lev, b_piece, b_lev, limit):
    keep = (
        (a_lev[:, :, None] > 0)
        & (b_lev[None, :, :] > 0)
        & (a_lev[:, :, None] + b_lev[None, :, :] <= limit[:, None, :])
    )
    counted = jnp.sum(keep.astype(jnp.int32), axis=1)
    results = []
    for column in range(limit.shape[1]):
        mask = jnp.repeat(keep[:, :, column], BLK, axis=0)
        masked = jnp.where(mask[None], a_piece, jnp.zeros((), jnp.bfloat16))
        right = b_piece[:, :, column * BLK : (column + 1) * BLK]
        real_real = jnp.dot(masked[0], right[0], preferred_element_type=jnp.float32)
        imag_imag = jnp.dot(masked[1], right[1], preferred_element_type=jnp.float32)
        real_imag = jnp.dot(masked[0], right[1], preferred_element_type=jnp.float32)
        imag_real = jnp.dot(masked[1], right[0], preferred_element_type=jnp.float32)
        results.append(jnp.stack([real_real - imag_imag, real_imag + imag_real]))
    return (jnp.concatenate(results, axis=2), counted)


def shards(a_matrix, b_matrix, a_level, b_level, limit):
    row_place = lax.axis_index("row")
    col_place = lax.axis_index("col")
    row_blocks = a_matrix.shape[1] // BLK
    col_blocks = a_matrix.shape[2] // BLK
    a_own = lax.dynamic_slice(
        a_level, (row_place * row_blocks, col_place * col_blocks), (row_blocks, col_blocks)
    )
    b_own = lax.dynamic_slice(
        b_level, (row_place * row_blocks, col_place * col_blocks), (row_blocks, col_blocks)
    )
    a_eff = a_matrix * spread_blocks(level_scale(a_own)).astype(jnp.bfloat16)[None]
    b_eff = b_matrix * spread_blocks(level_scale(b_own)).astype(jnp.bfloat16)[None]
    a_band = lax.dynamic_slice_in_dim(a_level, row_place * row_blocks, row_blocks, 0)
    b_band = lax.dynamic_slice_in_dim(b_level, col_place * col_blocks, col_blocks, 1)
    a_levels = jnp.repeat(a_band, BLK, axis=1)
    b_levels = jnp.repeat(b_band, BLK, axis=0)
    a_whole = lax.all_gather(a_eff, "col", axis=2, tiled=True)
    added, counted = block_terms(
        a_whole, a_levels, lax.all_gather(b_eff, "row", axis=1, tiled=True), b_levels, limit
    )
    kept_count = counted // BLK
    kept_total = lax.psum(jnp.sum(kept_count).reshape(1), ("row", "col"))
    return (added.astype(jnp.bfloat16), kept_count, kept_total)


def solution(mesh):
    in_specs = (
        P("kpt", "row", "col"),
        P("kpt", "row", "col"),
        P("kpt", None),
        P("kpt", None),
        P(("kpt", "row"), "col"),
    )
    out_specs = (P("kpt", "row", "col"), P(("kpt", "row"), "col"), P("kpt"))
    return jax.shard_map(shards, mesh=mesh, in_specs=in_specs, out_specs=out_specs, check_vma=False)
```

profile of v0, /device:TPU:0, one launch (start us, length us, event | category | flops | bytes accessed | tf_op | source)
XLA Modules:
  0.0 1229.6 jit_solution(12622931891409190300)
XLA Ops:
  25.3 8.4 broadcast_multiply_fusion
  37.7 14.6 %psum.7 = s32[1]{0:T(128)} all-reduce(s32[1]{0:T(128)} %bitcast.131), channel_id=1, replica_groups=mesh['kpt'=4,'row'=4,'col'=2] {'row','col'}, use_global_device_ids=true, to_apply=%region_2.3 | all-reduce | flops 1 | bytes 8 | tf_op jit(solution)/shard_map/psum | solution.py:60
  52.3 168.1 %all-gather.3.cloned.1.call-done = bf16[2,1024,4096]{2,1,0:T(8,128)(2,1)} async-done(((bf16[2,1024,2048]{2,1,0:T(8,128)(2,1)}), bf16[2,1024,4096]{2,1,0:T(8,128)(2,1)}) %all-gather.3.cloned.1.call-update) | async-done | bytes 16777232 | tf_op jit(solution)/shard_map/all_gather | solution.py:55
  285.2 115.4 %broadcast_select_fusion = (bf16[2,1024,4096]{2,1,0:T(8,128)(2,1)}, bf16[2,1024,4096]{2,1,0:T(8,128)(2,1)}, bf16[2,1024,4096]{2,1,0:T(8,128)(2,1)}, bf16[2,1024,...) fusion(bf16[2,1024,4096]{2,1,0:T(8,128)(2,1)} %all-gather.3.clo, ...), kind=kLoop, calls=%fused_computation | loop fusion | flops 134217728 | bytes 352321536 | tf_op jit(solution)/shard_map/jit(_where)/select_n | solution.py:28
  400.6 382.8 %all-gather.5.cloned.1.call-done = bf16[2,4096,2048]{2,1,0:T(8,128)(2,1)} async-done(((bf16[2,1024,2048]{2,1,0:T(8,128)(2,1)}), bf16[2,4096,2048]{2,1,0:T(8,128)(2,1)}) %all-gather.5.cloned.1.call-update) | async-done | bytes 33554448 | tf_op jit(solution)/shard_map/all_gather | solution.py:57
  783.4 6.7 fusion.1
  811.6 6.5 fusion.4
  818.1 6.7 fusion.157
  824.8 6.5 fusion.158
  832.1 6.5 fusion.9
  838.6 6.5 fusion.8
  845.2 6.5 fusion.155
  851.7 6.5 fusion.156
  859.0 6.7 fusion.13
  865.8 6.5 fusion.12
  872.3 6.5 fusion.153
  878.8 6.5 fusion.154
  886.1 6.5 fusion.17
  892.6 6.5 fusion.16
  899.2 6.9 fusion.151
  906.1 6.5 fusion.152
  913.4 6.5 fusion.21
  919.9 6.5 fusion.20
  926.5 6.5 fusion.149
  933.0 6.5 fusion.150
  940.3 6.7 fusion.25
  947.0 6.5 fusion.24
  953.5 6.5 fusion.147
  960.0 6.5 fusion.148
  967.4 6.5 fusion.29
  973.9 6.5 fusion.28
  980.4 6.7 fusion.145
  987.1 6.5 fusion.146
  1001.0 6.5 fusion.32
  1007.5 6.5 fusion.143
  1014.0 6.5 fusion.144
  1021.3 6.9 fusion.37
  1028.2 6.5 fusion.36
  1034.7 6.5 fusion.141
  1041.3 6.5 fusion.142
  1048.6 6.5 fusion.41
  1055.1 6.5 fusion.40
  1061.7 6.7 fusion.139
  1068.3 6.5 fusion.140
  1075.7 6.5 fusion.45
  1082.2 6.5 fusion.44
  1088.7 6.5 fusion.137
  1095.2 6.5 fusion.138
  1102.6 6.7 fusion.49
  1109.3 6.5 fusion.48
  1115.8 6.5 fusion.135
  1122.3 6.5 fusion.136
  1129.7 6.5 fusion.53
  1136.2 6.5 fusion.52
  1142.7 6.9 fusion.133
  1149.6 6.5 fusion.134
  1156.9 6.5 fusion.57
  1163.4 6.5 fusion.56
  1170.0 6.5 fusion.131
  1176.5 6.5 fusion.132
  1190.3 6.7 fusion.60
  1197.0 6.5 fusion.129
  1203.5 6.5 fusion.130
  1210.9 11.6 copy.28
  (72 shorter events, 133.7 us)
Async XLA Ops:
  7.2 213.3 %all-gather.3.cloned.1.call-start = ((), (), s32[]{:S(2)}) async-start(), calls=%async_computation | async-start | bytes 25165824 | tf_op jit(solution)/shard_map/all_gather | solution.py:55
  7.2 7.6 copy-start.1
  18.6 764.8 %all-gather.5.cloned.1.call-start = ((), (), s32[]{:S(2)}) async-start(), calls=%async_computation.1 | async-start | bytes 41943040 | tf_op jit(solution)/shard_map/all_gather | solution.py:57
  25.3 8.4 copy-start.2
  25.3 9.6 copy-start.3
  783.4 8.5 copy-start
Sparse Core Ops, SparseCore 0:
  18.7 201.6 all-gather.2
  222.0 561.3 all-gather.4
where the time goes:
time: 1240 us; the launch traced here: 1230 us
  waiting for transfers between devices  551 us (44%)
  matrix products  412 us (33%)
  other arithmetic  144 us (12%)
  local copies, waits for them, and re-layouts  92.9 us (7%)
  between operations  14.8 us (1%)
  blocking collectives  14.6 us (1%)
    all_gather x1, waiting for transfers between devices, shards(): lax.all_gather(b_eff, 'row', axis=1, tiled=True)  383 us
    all_gather x1, waiting for transfers between devices, shards(): a_whole = lax.all_gather(a_eff, 'col', axis=2, tiled=True)  168 us
    select_n x1, other arithmetic, block_terms(): masked = jnp.where(mask[None], a_piece, jnp.zeros((), jnp.bfloat16))  115 us
    dot_general x16, matrix products, block_terms(): real_real = jnp.dot(masked[0], right[0], preferred_element_type=jnp.float32)  105 us
    dot_general x16, matrix products, block_terms(): imag_imag = jnp.dot(masked[1], right[1], preferred_element_type=jnp.float32)  103 us
    dot_general x16, matrix products, block_terms(): real_imag = jnp.dot(masked[0], right[1], preferred_element_type=jnp.float32)  102 us
    dot_general x16, matrix products, block_terms(): imag_real = jnp.dot(masked[1], right[0], preferred_element_type=jnp.float32)  102 us
    broadcast_in_dim x16, local copies, waits for them, and re-layouts, block_terms(): mask = jnp.repeat(keep[:, :, column], BLK, axis=0)  64.8 us
  transfers between devices with their start and end apart: 2, of which 2 were waited for; matrix products, arithmetic and copies ran while one was open for 16% of the time, Pallas kernels for 0%

commit v1 on v0

--- a/solution.py
+++ b/solution.py
@@ -4,6 +4,27 @@
 from jax.sharding import PartitionSpec as P
 
 BLK = 128
+
+
+def ring_gather(value, axis, dim):
+    size, index, rows = (lax.axis_size(axis), lax.axis_index(axis), value.shape[dim])
+    ahead = [(i, (i + 1) % size) for i in range(size)]
+    behind = [(i, (i - 1) % size) for i in range(size)]
+    out = jnp.zeros((*value.shape[:dim], size * rows, *value.shape[dim + 1 :]), value.dtype)
+    out = lax.dynamic_update_slice_in_dim(out, value, index * rows, axis=dim)
+    from_left = from_right = value
+    halfway = size // 2
+    for step in range(1, halfway + 1):
+        from_left = lax.ppermute(from_left, axis, ahead)
+        out = lax.dynamic_update_slice_in_dim(
+            out, from_left, (index - step) % size * rows, axis=dim
+        )
+        if step < size - halfway:
+            from_right = lax.ppermute(from_right, axis, behind)
+            out = lax.dynamic_update_slice_in_dim(
+                out, from_right, (index + step) % size * rows, axis=dim
+            )
+    return out
 
 
 def level_scale(levels):
@@ -53,9 +74,7 @@
     a_levels = jnp.repeat(a_band, BLK, axis=1)
     b_levels = jnp.repeat(b_band, BLK, axis=0)
     a_whole = lax.all_gather(a_eff, "col", axis=2, tiled=True)
-    added, counted = block_terms(
-        a_whole, a_levels, lax.all_gather(b_eff, "row", axis=1, tiled=True), b_levels, limit
-    )
+    added, counted = block_terms(a_whole, a_levels, ring_gather(b_eff, "row", 1), b_levels, limit)
     kept_count = counted // BLK
     kept_total = lax.psum(jnp.sum(kept_count).reshape(1), ("row", "col"))
     return (added.astype(jnp.bfloat16), kept_count, kept_total)

time: 1240 us -> 1230 us (level)
  waiting for transfers between devices: 551 us -> 171 us
  blocking collectives: 14.6 us -> 357 us
  local copies, waits for them, and re-layouts: 92.9 us -> 132 us
  matrix products: 412 us -> 392 us
    all_gather x1 -> x0, waiting for transfers between devices: 383 us -> none  [shards(): lax.all_gather(b_eff, 'row', axis=1, tiled=True)]
    psum x1, blocking collectives: 14.6 us -> 357 us  [shards(): kept_total = lax.psum(jnp.sum(kept_count).reshape(1), ('row', 'col'))]
    ppermute x0 -> x3, waiting for transfers between devices: none -> 171 us  [the longest x2 171 us: ring_gather(): from_left = lax.ppermute(from_left, axis, ahead)]
    all_gather x1, waiting for transfers between devices: 168 us -> 0.01 us  [shards(): a_whole = lax.all_gather(a_eff, 'col', axis=2, tiled=True)]
    dynamic_update_slice x0 -> x3, local copies, waits for them, and re-layouts: none -> 25.2 us  [the longest x2 16.7 us: ring_gather(): lax.dynamic_update_slice_in_dim(out, from_left, (index - step) % size * r...]
    broadcast_in_dim x0 -> x1, local copies, waits for them, and re-layouts: none -> 13.1 us  [ring_gather(): jnp.zeros((*value.shape[:dim], size * rows, *value.shape[dim + 1:]), valu...]
  transfers between devices with their start and end apart: 2 -> 4, of which waited for: 2 -> 1; matrix products, arithmetic and copies ran while one was open for 16% -> 3% of each run, Pallas kernels for 0% -> 0%
where the time goes in v1:
time: 1230 us; the launch traced here: 1220 us
  matrix products  392 us (32%)
  blocking collectives  357 us (29%)
  waiting for transfers between devices  171 us (14%)
  other arithmetic  146 us (12%)
  local copies, waits for them, and re-layouts  132 us (11%)
  between operations  15.7 us (1%)
    psum x1, blocking collectives, shards(): kept_total = lax.psum(jnp.sum(kept_count).reshape(1), ('row', 'col'))  357 us
    ppermute x2, waiting for transfers between devices, ring_gather(): from_left = lax.ppermute(from_left, axis, ahead)  171 us
    select_n x1, other arithmetic, block_terms(): masked = jnp.where(mask[None], a_piece, jnp.zeros((), jnp.bfloat16))  115 us
    dot_general x16, matrix products, block_terms(): imag_imag = jnp.dot(masked[1], right[1], preferred_element_type=jnp.float32)  104 us
    dot_general x16, matrix products, block_terms(): real_real = jnp.dot(masked[0], right[0], preferred_element_type=jnp.float32)  99.3 us
    dot_general x16, matrix products, block_terms(): imag_real = jnp.dot(masked[1], right[0], preferred_element_type=jnp.float32)  96.1 us
    dot_general x16, matrix products, block_terms(): real_imag = jnp.dot(masked[0], right[1], preferred_element_type=jnp.float32)  92 us
    broadcast_in_dim x16, local copies, waits for them, and re-layouts, block_terms(): mask = jnp.repeat(keep[:, :, column], BLK, axis=0)  63.2 us
  transfers between devices with their start and end apart: 4, of which 1 were waited for; matrix products, arithmetic and copies ran while one was open for 3% of the time, Pallas kernels for 0%

profile of v1, /device:TPU:0, one launch (start us, length us, event | category | flops | bytes accessed | tf_op | source)
XLA Modules:
  0.0 1219.5 jit_solution(17507505233976370654)
XLA Ops:
  16.7 13.1 %broadcast_in_dim.220 = bf16[2,4096,2048]{2,1,0:T(8,128)(2,1)} broadcast(bf16[]{:T(256)} %constant.62.clone.1), dimensions={} | broadcast | bytes 33554432 | tf_op jit(solution)/shard_map/broadcast_in_dim | solution.py:13
  29.8 11.0 constant_dynamic-update-slice_fusion.3
  56.4 171.1 %collective-permute-done = bf16[2,1024,2048]{2,1,0:T(8,128)(2,1)} collective-permute-done((bf16[2,1024,2048]{2,1,0:T(8,128)(2,1)}, bf16[2,1024,2048]{2,1,0:T(8,128)(2,1)}, u32[]{:S(2)}, u32[]{:S(2)}) %collective-permute-start) | collective-permute-done | bytes 8388640 | tf_op jit(solution)/shard_map/ppermute | solution.py:18
  231.5 357.4 %psum.7 = s32[1]{0:T(128)} all-reduce(s32[1]{0:T(128)} %bitcast.131), channel_id=1, replica_groups=mesh['kpt'=4,'row'=4,'col'=2] {'row','col'}, use_global_device_ids=true, to_apply=%region_2.3 | all-reduce | flops 1 | bytes 8 | tf_op jit(solution)/shard_map/psum | solution.py:79
  589.0 8.3 constant_dynamic-update-slice_fusion.2
  597.3 8.5 constant_dynamic-update-slice_fusion.1
  605.8 8.4 constant_dynamic-update-slice_fusion
  677.5 114.7 %broadcast_select_fusion = (bf16[2,1024,4096]{2,1,0:T(8,128)(2,1)}, bf16[2,1024,4096]{2,1,0:T(8,128)(2,1)}, bf16[2,1024,4096]{2,1,0:T(8,128)(2,1)}, bf16[2,1024,...) fusion(bf16[2,1024,4096]{2,1,0:T(8,128)(2,1)} %all-gather.2.clo, ...), kind=kLoop, calls=%fused_computation | loop fusion | flops 134217728 | bytes 352321536 | tf_op jit(solution)/shard_map/jit(_where)/select_n | solution.py:49
  792.2 7.5 fusion.2
  800.8 4.9 fusion.3
  805.8 7.5 fusion.6
  813.3 7.5 fusion.7
  820.8 5.1 fusion.10
  825.9 7.5 fusion.11
  833.4 5.1 fusion.14
  838.4 4.9 fusion.15
  843.4 7.5 fusion.18
  850.9 7.5 fusion.19
  858.4 5.1 fusion.22
  863.5 7.5 fusion.23
  871.0 5.1 fusion.26
  876.1 4.9 fusion.27
  881.1 7.5 fusion.30
  888.5 7.4 fusion.31
  896.0 5.1 fusion.34
  901.1 7.5 fusion.35
  908.6 5.3 fusion.38
  913.9 4.9 fusion.39
  918.9 7.5 fusion.42
  926.3 7.5 fusion.43
  933.9 5.1 fusion.46
  939.0 7.5 fusion.47
  946.4 5.1 fusion.50
  951.5 4.9 fusion.51
  956.5 7.5 fusion.54
  964.0 7.5 fusion.55
  971.5 5.1 fusion.58
  976.6 7.5 fusion.59
  984.1 5.2 fusion.62
  989.3 5.1 fusion.63
  994.4 7.4 fusion.160
  1001.8 4.9 fusion.159
  1006.7 7.4 fusion.158
  1014.1 6.7 fusion.157
  1025.6 6.7 fusion.155
  1040.7 6.7 fusion.152
  1047.4 6.7 fusion.151
  1058.8 7.5 fusion.149
  1066.3 4.9 fusion.148
  1076.1 7.4 fusion.146
  1083.4 7.4 fusion.145
  1090.9 5.3 fusion.144
  1096.2 7.5 fusion.143
  1103.8 4.9 fusion.142
  1113.6 7.4 fusion.140
  1121.0 7.4 fusion.139
  1128.4 5.5 fusion.138
  1134.0 7.5 fusion.137
  1141.5 4.9 fusion.136
  1151.3 7.4 fusion.134
  1158.7 7.4 fusion.133
  1166.1 5.3 fusion.132
  1171.4 6.8 fusion.131
  1200.9 11.6 copy.28
  (363 shorter events, 148.4 us)
Async XLA Ops:
  7.2 607.1 %all-gather.2.cloned.1.call-start = ((), (), s32[]{:S(2)}) async-start(), calls=%async_computation | async-start | bytes 25165824 | tf_op jit(solution)/shard_map/all_gather | solution.py:76
  16.6 13.2 %copy-start = (bf16[128,8,16,128]{3,1,2,0:T(8,128)(2,1)S(1)}, bf16[128,8,16,128]{3,1,2,0:T(8,128)(2,1)}, u32[]{:S(2)}) copy-start(bf16[128,8,16,128]{3,1,2,0:T(8,128)(2,1)} %copy.37) | copy-start | bytes 12582916
  16.6 34.0 %slice-start.84 = ((s8[8388608]{0:T(1024)(128)(4,1)}), s8[4194304]{0:T(1024)(128)(4,1)S(1)}, s32[]{:S(2)}) async-start(s8[8388608]{0:T(1024)(128)(4,1)} %bitcast.644), calls=%async_computation.85 | async-start | bytes 8388608
  29.8 20.9 %slice-start.85 = ((s8[8388608]{0:T(1024)(128)(4,1)}), s8[4194304]{0:T(1024)(128)(4,1)S(1)}, s32[]{:S(2)}) async-start(s8[8388608]{0:T(1024)(128)(4,1)} %bitcast.644), calls=%async_computation.86 | async-start | bytes 8388608
  40.8 186.7 %collective-permute-start = (bf16[2,1024,2048]{2,1,0:T(8,128)(2,1)}, bf16[2,1024,2048]{2,1,0:T(8,128)(2,1)}, u32[]{:S(2)}, u32[]{:S(2)}) collective-permute-start(bf16[2,1024,2048]{2,1,0:T(8,128)(2,1)} %get-tuple-element.17), channel_id=1, source_target_pairs={{0,2},{2,4},{4,6},{6,0},{1,3},{3,5},{5,7},{7,1},{8,10},{10,12},{12... | collective-permute-start | bytes 25165832 | tf_op jit(solution)/shard_map/ppermute | solution.py:18
  50.6 177.0 %copy-start.24 = (s32[8,16]{1,0:T(8,128)S(1)}, s32[8,16]{1,0:T(8,128)}, u32[]{:S(2)}) copy-start(s32[8,16]{1,0:T(8,128)} %param.9) | copy-start | bytes 1540
  50.6 177.1 %copy-start.23 = (s32[32,32]{1,0:T(8,128)S(1)}, s32[32,32]{1,0:T(8,128)}, u32[]{:S(2)}) copy-start(s32[32,32]{1,0:T(8,128)} %param.8) | copy-start | bytes 12292
  54.5 542.8 %collective-permute-start.1 = (bf16[2,1024,2048]{2,1,0:T(8,128)(2,1)}, bf16[2,1024,2048]{2,1,0:T(8,128)(2,1)}, u32[]{:S(2)}, u32[]{:S(2)}) collective-permute-start(bf16[2,1024,2048]{2,1,0:T(8,128)(2,1)} %get-tuple-element.17), channel_id=1, source_target_pairs={{0,6},{2,0},{4,2},{6,4},{1,7},{3,1},{5,3},{7,5},{8,14},{10,8},{12,... | collective-permute-start | bytes 25165832 | tf_op jit(solution)/shard_map/ppermute | solution.py:23
  227.5 378.3 %collective-permute-start.2 = (bf16[2,1024,2048]{2,1,0:T(8,128)(2,1)}, bf16[2,1024,2048]{2,1,0:T(8,128)(2,1)}, u32[]{:S(2)}, u32[]{:S(2)}) collective-permute-start(bf16[2,1024,2048]{2,1,0:T(8,128)(2,1)} %collective-permute-done), channel_id=1, source_target_pairs={{0,2},{2,4},{4,6},{6,0},{1,3},{3,5},{5,7},{7,1},{8,10},{10,12},{12... | collective-permute-start | bytes 25165832 | tf_op jit(solution)/shard_map/ppermute | solution.py:18
  805.8 15.0 %slice-start.72 = ((s8[16777216]{0:T(1024)(128)(4,1)}), s8[4194304]{0:T(1024)(128)(4,1)S(1)}, s32[]{:S(2)}) async-start(s8[16777216]{0:T(1024)(128)(4,1)} %bitcast.638), calls=%async_computation.73 | async-start | bytes 8388608
  805.8 15.0 %slice-start.73 = ((s8[16777216]{0:T(1024)(128)(4,1)}), s8[4194304]{0:T(1024)(128)(4,1)S(1)}, s32[]{:S(2)}) async-start(s8[16777216]{0:T(1024)(128)(4,1)} %bitcast.638), calls=%async_computation.74 | async-start | bytes 8388608
  820.7 12.6 %slice-start.64 = ((s8[16777216]{0:T(1024)(128)(4,1)}), s8[4194304]{0:T(1024)(128)(4,1)S(1)}, s32[]{:S(2)}) async-start(s8[16777216]{0:T(1024)(128)(4,1)} %bitcast.634), calls=%async_computation.65 | async-start | bytes 8388608
  820.8 12.6 %slice-start.65 = ((s8[16777216]{0:T(1024)(128)(4,1)}), s8[4194304]{0:T(1024)(128)(4,1)S(1)}, s32[]{:S(2)}) async-start(s8[16777216]{0:T(1024)(128)(4,1)} %bitcast.634), calls=%async_computation.66 | async-start | bytes 8388608
  843.4 15.0 %slice-start.56 = ((s8[16777216]{0:T(1024)(128)(4,1)}), s8[4194304]{0:T(1024)(128)(4,1)S(1)}, s32[]{:S(2)}) async-start(s8[16777216]{0:T(1024)(128)(4,1)} %bitcast.630), calls=%async_computation.57 | async-start | bytes 8388608
  843.4 15.0 %slice-start.57 = ((s8[16777216]{0:T(1024)(128)(4,1)}), s8[4194304]{0:T(1024)(128)(4,1)S(1)}, s32[]{:S(2)}) async-start(s8[16777216]{0:T(1024)(128)(4,1)} %bitcast.630), calls=%async_computation.58 | async-start | bytes 8388608
  858.4 12.6 %slice-start.48 = ((s8[16777216]{0:T(1024)(128)(4,1)}), s8[4194304]{0:T(1024)(128)(4,1)S(1)}, s32[]{:S(2)}) async-start(s8[16777216]{0:T(1024)(128)(4,1)} %bitcast.626), calls=%async_computation.49 | async-start | bytes 8388608
  858.4 12.6 %slice-start.49 = ((s8[16777216]{0:T(1024)(128)(4,1)}), s8[4194304]{0:T(1024)(128)(4,1)S(1)}, s32[]{:S(2)}) async-start(s8[16777216]{0:T(1024)(128)(4,1)} %bitcast.626), calls=%async_computation.50 | async-start | bytes 8388608
  881.1 14.9 %slice-start.40 = ((s8[16777216]{0:T(1024)(128)(4,1)}), s8[4194304]{0:T(1024)(128)(4,1)S(1)}, s32[]{:S(2)}) async-start(s8[16777216]{0:T(1024)(128)(4,1)} %bitcast.622), calls=%async_computation.41 | async-start | bytes 8388608
  881.1 14.9 %slice-start.41 = ((s8[16777216]{0:T(1024)(128)(4,1)}), s8[4194304]{0:T(1024)(128)(4,1)S(1)}, s32[]{:S(2)}) async-start(s8[16777216]{0:T(1024)(128)(4,1)} %bitcast.622), calls=%async_computation.42 | async-start | bytes 8388608
  896.0 12.6 %slice-start.32 = ((s8[16777216]{0:T(1024)(128)(4,1)}), s8[4194304]{0:T(1024)(128)(4,1)S(1)}, s32[]{:S(2)}) async-start(s8[16777216]{0:T(1024)(128)(4,1)} %bitcast.618), calls=%async_computation.33 | async-start | bytes 8388608
  896.0 12.6 %slice-start.33 = ((s8[16777216]{0:T(1024)(128)(4,1)}), s8[4194304]{0:T(1024)(128)(4,1)S(1)}, s32[]{:S(2)}) async-start(s8[16777216]{0:T(1024)(128)(4,1)} %bitcast.618), calls=%async_computation.34 | async-start | bytes 8388608
  918.9 14.9 %slice-start.24 = ((s8[16777216]{0:T(1024)(128)(4,1)}), s8[4194304]{0:T(1024)(128)(4,1)S(1)}, s32[]{:S(2)}) async-start(s8[16777216]{0:T(1024)(128)(4,1)} %bitcast.614), calls=%async_computation.25 | async-start | bytes 8388608
  918.9 14.9 %slice-start.25 = ((s8[16777216]{0:T(1024)(128)(4,1)}), s8[4194304]{0:T(1024)(128)(4,1)S(1)}, s32[]{:S(2)}) async-start(s8[16777216]{0:T(1024)(128)(4,1)} %bitcast.614), calls=%async_computation.26 | async-start | bytes 8388608
  933.8 12.6 %slice-start.16 = ((s8[16777216]{0:T(1024)(128)(4,1)}), s8[4194304]{0:T(1024)(128)(4,1)S(1)}, s32[]{:S(2)}) async-start(s8[16777216]{0:T(1024)(128)(4,1)} %bitcast.610), calls=%async_computation.17 | async-start | bytes 8388608
  933.8 12.6 %slice-start.17 = ((s8[16777216]{0:T(1024)(128)(4,1)}), s8[4194304]{0:T(1024)(128)(4,1)S(1)}, s32[]{:S(2)}) async-start(s8[16777216]{0:T(1024)(128)(4,1)} %bitcast.610), calls=%async_computation.18 | async-start | bytes 8388608
  956.5 15.0 %slice-start.8 = ((s8[16777216]{0:T(1024)(128)(4,1)}), s8[4194304]{0:T(1024)(128)(4,1)S(1)}, s32[]{:S(2)}) async-start(s8[16777216]{0:T(1024)(128)(4,1)} %bitcast.606), calls=%async_computation.9 | async-start | bytes 8388608
  956.5 15.0 %slice-start.9 = ((s8[16777216]{0:T(1024)(128)(4,1)}), s8[4194304]{0:T(1024)(128)(4,1)S(1)}, s32[]{:S(2)}) async-start(s8[16777216]{0:T(1024)(128)(4,1)} %bitcast.606), calls=%async_computation.10 | async-start | bytes 8388608
  971.5 12.6 %slice-start = ((s8[16777216]{0:T(1024)(128)(4,1)}), s8[4194304]{0:T(1024)(128)(4,1)S(1)}, s32[]{:S(2)}) async-start(s8[16777216]{0:T(1024)(128)(4,1)} %bitcast.602), calls=%async_computation.1 | async-start | bytes 8388608
  971.5 12.5 %slice-start.1 = ((s8[16777216]{0:T(1024)(128)(4,1)}), s8[4194304]{0:T(1024)(128)(4,1)S(1)}, s32[]{:S(2)}) async-start(s8[16777216]{0:T(1024)(128)(4,1)} %bitcast.602), calls=%async_computation.2 | async-start | bytes 8388608
  989.3 12.5 %slice-start.80 = ((s8[16777216]{0:T(1024)(128)(4,1)}), s8[4194304]{0:T(1024)(128)(4,1)S(1)}, s32[]{:S(2)}) async-start(s8[16777216]{0:T(1024)(128)(4,1)} %bitcast.642), calls=%async_computation.81 | async-start | bytes 8388608
  989.3 12.5 %slice-start.81 = ((s8[16777216]{0:T(1024)(128)(4,1)}), s8[4194304]{0:T(1024)(128)(4,1)S(1)}, s32[]{:S(2)}) async-start(s8[16777216]{0:T(1024)(128)(4,1)} %bitcast.642), calls=%async_computation.82 | async-start | bytes 8388608
  989.3 12.5 %copy-start.47 = (f32[1024,128]{0,1:T(8,128)S(1)}, f32[1024,128]{0,1:T(8,128)}, u32[]{:S(2)}) copy-start(f32[1024,128]{0,1:T(8,128)} %fusion.3) | copy-start | bytes 1572868
  994.4 12.3 %copy-start.46 = (f32[1024,128]{0,1:T(8,128)S(1)}, f32[1024,128]{0,1:T(8,128)}, u32[]{:S(2)}) copy-start(f32[1024,128]{0,1:T(8,128)} %fusion.6) | copy-start | bytes 1572868
  1001.8 12.3 %copy-start.45 = (f32[1024,128]{0,1:T(8,128)S(1)}, f32[1024,128]{0,1:T(8,128)}, u32[]{:S(2)}) copy-start(f32[1024,128]{0,1:T(8,128)} %fusion.7) | copy-start | bytes 1572868
  1006.7 14.1 %slice-start.76 = ((s8[16777216]{0:T(1024)(128)(4,1)}), s8[4194304]{0:T(1024)(128)(4,1)S(1)}, s32[]{:S(2)}) async-start(s8[16777216]{0:T(1024)(128)(4,1)} %bitcast.640), calls=%async_computation.77 | async-start | bytes 8388608
  1006.7 14.1 %slice-start.77 = ((s8[16777216]{0:T(1024)(128)(4,1)}), s8[4194304]{0:T(1024)(128)(4,1)S(1)}, s32[]{:S(2)}) async-start(s8[16777216]{0:T(1024)(128)(4,1)} %bitcast.640), calls=%async_computation.78 | async-start | bytes 8388608
  1006.7 14.1 %copy-start.44 = (f32[1024,128]{0,1:T(8,128)S(1)}, f32[1024,128]{0,1:T(8,128)}, u32[]{:S(2)}) copy-start(f32[1024,128]{0,1:T(8,128)} %fusion.10) | copy-start | bytes 1572868
  1040.7 13.4 %slice-start.60 = ((s8[16777216]{0:T(1024)(128)(4,1)}), s8[4194304]{0:T(1024)(128)(4,1)S(1)}, s32[]{:S(2)}) async-start(s8[16777216]{0:T(1024)(128)(4,1)} %bitcast.632), calls=%async_computation.61 | async-start | bytes 8388608
  1040.7 13.4 %slice-start.61 = ((s8[16777216]{0:T(1024)(128)(4,1)}), s8[4194304]{0:T(1024)(128)(4,1)S(1)}, s32[]{:S(2)}) async-start(s8[16777216]{0:T(1024)(128)(4,1)} %bitcast.632), calls=%async_computation.62 | async-start | bytes 8388608
  1058.8 12.4 %copy-start.37 = (f32[1024,128]{0,1:T(8,128)S(1)}, f32[1024,128]{0,1:T(8,128)}, u32[]{:S(2)}) copy-start(f32[1024,128]{0,1:T(8,128)} %fusion.27) | copy-start | bytes 1572868
  1076.1 14.8 %slice-start.44 = ((s8[16777216]{0:T(1024)(128)(4,1)}), s8[4194304]{0:T(1024)(128)(4,1)S(1)}, s32[]{:S(2)}) async-start(s8[16777216]{0:T(1024)(128)(4,1)} %bitcast.624), calls=%async_computation.45 | async-start | bytes 8388608
  1076.1 14.8 %slice-start.45 = ((s8[16777216]{0:T(1024)(128)(4,1)}), s8[4194304]{0:T(1024)(128)(4,1)S(1)}, s32[]{:S(2)}) async-start(s8[16777216]{0:T(1024)(128)(4,1)} %bitcast.624), calls=%async_computation.46 | async-start | bytes 8388608
  1090.9 12.9 %slice-start.36 = ((s8[16777216]{0:T(1024)(128)(4,1)}), s8[4194304]{0:T(1024)(128)(4,1)S(1)}, s32[]{:S(2)}) async-start(s8[16777216]{0:T(1024)(128)(4,1)} %bitcast.620), calls=%async_computation.37 | async-start | bytes 8388608
  1090.9 12.9 %slice-start.37 = ((s8[16777216]{0:T(1024)(128)(4,1)}), s8[4194304]{0:T(1024)(128)(4,1)S(1)}, s32[]{:S(2)}) async-start(s8[16777216]{0:T(1024)(128)(4,1)} %bitcast.620), calls=%async_computation.38 | async-start | bytes 8388608
  1096.2 12.5 %copy-start.33 = (f32[1024,128]{0,1:T(8,128)S(1)}, f32[1024,128]{0,1:T(8,128)}, u32[]{:S(2)}) copy-start(f32[1024,128]{0,1:T(8,128)} %fusion.39) | copy-start | bytes 1572868
  1113.6 14.8 %slice-start.28 = ((s8[16777216]{0:T(1024)(128)(4,1)}), s8[4194304]{0:T(1024)(128)(4,1)S(1)}, s32[]{:S(2)}) async-start(s8[16777216]{0:T(1024)(128)(4,1)} %bitcast.616), calls=%async_computation.29 | async-start | bytes 8388608
  1113.6 14.8 %slice-start.29 = ((s8[16777216]{0:T(1024)(128)(4,1)}), s8[4194304]{0:T(1024)(128)(4,1)S(1)}, s32[]{:S(2)}) async-start(s8[16777216]{0:T(1024)(128)(4,1)} %bitcast.616), calls=%async_computation.30 | async-start | bytes 8388608
  1128.4 13.1 %slice-start.20 = ((s8[16777216]{0:T(1024)(128)(4,1)}), s8[4194304]{0:T(1024)(128)(4,1)S(1)}, s32[]{:S(2)}) async-start(s8[16777216]{0:T(1024)(128)(4,1)} %bitcast.612), calls=%async_computation.21 | async-start | bytes 8388608
  1128.4 13.1 %slice-start.21 = ((s8[16777216]{0:T(1024)(128)(4,1)}), s8[4194304]{0:T(1024)(128)(4,1)S(1)}, s32[]{:S(2)}) async-start(s8[16777216]{0:T(1024)(128)(4,1)} %bitcast.612), calls=%async_computation.22 | async-start | bytes 8388608
  1134.0 12.4 %copy-start.29 = (f32[1024,128]{0,1:T(8,128)S(1)}, f32[1024,128]{0,1:T(8,128)}, u32[]{:S(2)}) copy-start(f32[1024,128]{0,1:T(8,128)} %fusion.51) | copy-start | bytes 1572868
  1151.3 14.8 %slice-start.12 = ((s8[16777216]{0:T(1024)(128)(4,1)}), s8[4194304]{0:T(1024)(128)(4,1)S(1)}, s32[]{:S(2)}) async-start(s8[16777216]{0:T(1024)(128)(4,1)} %bitcast.608), calls=%async_computation.13 | async-start | bytes 8388608
  1151.3 14.8 %slice-start.13 = ((s8[16777216]{0:T(1024)(128)(4,1)}), s8[4194304]{0:T(1024)(128)(4,1)S(1)}, s32[]{:S(2)}) async-start(s8[16777216]{0:T(1024)(128)(4,1)} %bitcast.608), calls=%async_computation.14 | async-start | bytes 8388608
  1178.3 12.9 %copy-start.5 = (bf16[1,1024,128]{1,2,0:T(8,128)(2,1)S(1)}, bf16[1,1024,128]{1,2,0:T(8,128)(2,1)}, u32[]{:S(2)}) copy-start(bf16[1,1024,128]{1,2,0:T(8,128)(2,1)} %fusion.149) | copy-start | bytes 786436
  1182.6 12.2 %copy-start.12 = (bf16[1,1024,128]{1,2,0:T(8,128)(2,1)S(1)}, bf16[1,1024,128]{1,2,0:T(8,128)(2,1)}, u32[]{:S(2)}) copy-start(bf16[1,1024,128]{1,2,0:T(8,128)(2,1)} %fusion.142) | copy-start | bytes 786436
  1182.6 12.2 %copy-start.13 = (bf16[1,1024,128]{1,2,0:T(8,128)(2,1)S(1)}, bf16[1,1024,128]{1,2,0:T(8,128)(2,1)}, u32[]{:S(2)}) copy-start(bf16[1,1024,128]{1,2,0:T(8,128)(2,1)} %fusion.141) | copy-start | bytes 786436
  1182.6 13.1 %copy-start.14 = (bf16[1,1024,128]{1,2,0:T(8,128)(2,1)S(1)}, bf16[1,1024,128]{1,2,0:T(8,128)(2,1)}, u32[]{:S(2)}) copy-start(bf16[1,1024,128]{1,2,0:T(8,128)(2,1)} %fusion.140) | copy-start | bytes 786436
  1182.6 13.0 %copy-start.15 = (bf16[1,1024,128]{1,2,0:T(8,128)(2,1)S(1)}, bf16[1,1024,128]{1,2,0:T(8,128)(2,1)}, u32[]{:S(2)}) copy-start(bf16[1,1024,128]{1,2,0:T(8,128)(2,1)} %fusion.139) | copy-start | bytes 786436
  1182.6 13.9 %copy-start.16 = (bf16[1,1024,128]{1,2,0:T(8,128)(2,1)S(1)}, bf16[1,1024,128]{1,2,0:T(8,128)(2,1)}, u32[]{:S(2)}) copy-start(bf16[1,1024,128]{1,2,0:T(8,128)(2,1)} %fusion.138) | copy-start | bytes 786436
  1182.6 13.9 %copy-start.17 = (bf16[1,1024,128]{1,2,0:T(8,128)(2,1)S(1)}, bf16[1,1024,128]{1,2,0:T(8,128)(2,1)}, u32[]{:S(2)}) copy-start(bf16[1,1024,128]{1,2,0:T(8,128)(2,1)} %fusion.137) | copy-start | bytes 786436
  1182.7 14.8 %copy-start.18 = (bf16[1,1024,128]{1,2,0:T(8,128)(2,1)S(1)}, bf16[1,1024,128]{1,2,0:T(8,128)(2,1)}, u32[]{:S(2)}) copy-start(bf16[1,1024,128]{1,2,0:T(8,128)(2,1)} %fusion.136) | copy-start | bytes 786436
  1182.7 14.8 %copy-start.19 = (bf16[1,1024,128]{1,2,0:T(8,128)(2,1)S(1)}, bf16[1,1024,128]{1,2,0:T(8,128)(2,1)}, u32[]{:S(2)}) copy-start(bf16[1,1024,128]{1,2,0:T(8,128)(2,1)} %fusion.135) | copy-start | bytes 786436
  1182.7 15.7 %copy-start.20 = (bf16[1,1024,128]{1,2,0:T(8,128)(2,1)S(1)}, bf16[1,1024,128]{1,2,0:T(8,128)(2,1)}, u32[]{:S(2)}) copy-start(bf16[1,1024,128]{1,2,0:T(8,128)(2,1)} %fusion.134) | copy-start | bytes 786436
  1182.7 15.7 %copy-start.21 = (bf16[1,1024,128]{1,2,0:T(8,128)(2,1)S(1)}, bf16[1,1024,128]{1,2,0:T(8,128)(2,1)}, u32[]{:S(2)}) copy-start(bf16[1,1024,128]{1,2,0:T(8,128)(2,1)} %fusion.133) | copy-start | bytes 786436
  1182.7 16.5 %copy-start.22 = (bf16[1,1024,128]{1,2,0:T(8,128)(2,1)S(1)}, bf16[1,1024,128]{1,2,0:T(8,128)(2,1)}, u32[]{:S(2)}) copy-start(bf16[1,1024,128]{1,2,0:T(8,128)(2,1)} %fusion.132) | copy-start | bytes 786436
  (75 other events, 629.2 us)
Sparse Core Ops, SparseCore 0:
  54.6 198.9 all-gather.1
